TPU v7x, 32 devices: a whole 2x2x4 slice. The times are simulated.
32 devices in a mesh: dp: 8 (over z, y), tensor: 4 (over x, core).
Axes of the slice: x: 2, y: 2, z: 4, core: 2. Of those that a mesh axis runs over, the one named last changes fastest.
Arguments:
- hidden_in: bfloat16 [4096, 1024], P(('dp', 'tensor')), may hold values from -5 to 5
- cotangent: bfloat16 [4096, 1024], P(('dp', 'tensor')), may hold values from -20 to 20
- segments: int32 [8, 512], P('dp'), may hold values from 0 to 3, as said below
- routes: int32 [4096, 8], P(('dp', 'tensor')), may hold values from 0 to 31, as said below
- gain_attn: float32 [1024], replicated, may hold values from 0.5 to 1.5
- w_query: bfloat16 [1024, 1024], P(None, 'tensor'), may hold values from -0.125 to 0.125
- key_matrix: bfloat16 [1024, 512], P(None, 'tensor'), may hold values from -0.125 to 0.125
- value_matrix: bfloat16 [1024, 512], P(None, 'tensor'), may hold values from -0.1875 to 0.1875
- attention_output_weight: bfloat16 [1024, 1024], P('tensor'), may hold values from -0.75 to 0.75
- gain_ffn: float32 [1024], replicated, may hold values from 0.5 to 1.5
- w_router: bfloat16 [1024, 32], replicated, may hold values from -0.34 to 0.34
- w_gate: bfloat16 [2, 1024, 512], P(None, None, 'tensor'), may hold values from -0.1875 to 0.1875
- w_up: bfloat16 [2, 1024, 512], P(None, None, 'tensor'), may hold values from -0.1875 to 0.1875
- w_down: bfloat16 [2, 512, 1024], P(None, 'tensor'), may hold values from -0.75 to 0.75
Outputs:
- output: bfloat16 [4096, 1024], P(('dp', 'tensor'))
- grad_in: float32 [4096, 1024], P(('dp', 'tensor'))
- grad_gain_attn: float32 [1024], replicated
- grad_w_query: float32 [1024, 1024], P(None, 'tensor')
- grad_w_key: float32 [1024, 512], P(None, 'tensor')
- grad_w_value: float32 [1024, 512], P(None, 'tensor')
- grad_w_out: float32 [1024, 1024], P('tensor')
- grad_gain_ffn: float32 [1024], replicated
- grad_router: float32 [1024, 32], replicated
- grad_gate: float32 [2, 1024, 512], P(None, None, 'tensor')
- grad_up: float32 [2, 1024, 512], P(None, None, 'tensor')
- grad_down: float32 [2, 512, 1024], P(None, 'tensor')
Inputs may be any that keep to these rules, and one draw needn't show every extreme that they name: `segments`: numbers start at 0 and rise by one at each new document along a packed sequence; a packed sequence holds 2 to 4 documents, each of 102 to 256 tokens. `routes`: each token names 8 different experts.
All inputs are finite; a program needn't handle non-finite values.
Results may differ from a plain program's by a relative error of at most 0.034.
Values may be sent and summed in bfloat16 or wider, within the bound.
A program may use at most 128 MiB of HBM per device.

v0:
```python
import jax
import jax.numpy as jnp
from jax import lax
from jax.sharding import PartitionSpec as P

HEAD_SIZE = 64


EPS = 1e-06
THETA = 10000.0
NEGATIVE = -1e30


def inner_rows(left_op, right_op):
    return lax.dot_general(
        left_op, right_op, (((0,), (0,)), ((), ())), preferred_element_type=jnp.float32
    )


def outer_columns(left_op, right_op):
    return lax.dot_general(
        left_op, right_op, (((1,), (1,)), ((), ())), preferred_element_type=jnp.float32
    )


def rotary_tables(sequence_rows):
    half_dim = HEAD_SIZE // 2
    freq_table = THETA ** (-(jnp.arange(half_dim).astype(jnp.float32) * 2.0 / HEAD_SIZE))
    angles = jnp.arange(sequence_rows).astype(jnp.float32)[:, None] * freq_table[None, :]
    return (jnp.cos(angles)[:, None, :], jnp.sin(angles)[:, None, :])


def apply_rotary(vals_in, cosine_table, sine_values, direction):
    half_dim = vals_in.shape[-1] // 2
    first_half = vals_in[..., :half_dim]
    second_half = vals_in[..., half_dim:]
    return jnp.concatenate(
        [
            first_half * cosine_table - direction * second_half * sine_values,
            second_half * cosine_table + direction * first_half * sine_values,
        ],
        axis=-1,
    )


def norm_forward(row_vals, gain_vec):
    inverse = lax.rsqrt(jnp.mean(row_vals * row_vals, axis=-1, keepdims=True) + EPS)
    normed = row_vals * inverse
    return ((normed * gain_vec).astype(jnp.bfloat16), normed, inverse)


def norm_backward(grad_out, normed, inverse, gain_vec):
    grad_gain = jnp.sum(grad_out * normed, axis=0)
    scaled = grad_out * gain_vec
    grad_rows = inverse * (scaled - normed * jnp.mean(scaled * normed, axis=-1, keepdims=True))
    return (grad_rows, grad_gain)


def gate_parts(gate_pre):
    sig_vals = jax.nn.sigmoid(gate_pre)
    return (gate_pre * sig_vals, sig_vals * (1.0 + gate_pre * (1.0 - sig_vals)))


def block_scores(query_block, keys_part, seg_row, row_start, row_stop):
    allowed = (seg_row[row_start:row_stop, None] == seg_row[None, :row_stop]) & (
        jnp.arange(row_stop)[None, :] <= jnp.arange(row_start, row_stop)[:, None]
    )
    scores = jnp.einsum(
        "qhgd,khd->hgqk", query_block, keys_part, preferred_element_type=jnp.float32
    ) * HEAD_SIZE ** (-0.5)
    return jnp.where(allowed[None, None], scores, NEGATIVE)


def on_device(
    hidden_in,
    cotangent,
    segments,
    routes,
    gain_attn,
    w_query,
    key_matrix,
    value_matrix,
    attention_output_weight,
    gain_ffn,
    w_router,
    w_gate,
    w_up,
    w_down,
):
    shard_rows = hidden_in.shape[0]
    width = hidden_in.shape[1]
    seg_row = segments[0]
    sequence_rows = seg_row.shape[0]
    kv_local = key_matrix.shape[1] // HEAD_SIZE
    heads_local = w_query.shape[1] // HEAD_SIZE
    query_groups = heads_local // kv_local
    experts_win = w_gate.shape[0]
    block_rows = min(512, sequence_rows)
    scale_factor = HEAD_SIZE ** (-0.5)
    cosine_table, sine_values = rotary_tables(sequence_rows)
    rows_in = hidden_in.astype(jnp.float32)
    attention_normed, unit_attn, inverse_attn = norm_forward(rows_in, gain_attn)
    full_attn = lax.all_gather(attention_normed, "tensor", axis=0, tiled=True)
    query_before_rotary = jnp.dot(full_attn, w_query, preferred_element_type=jnp.float32).reshape(
        sequence_rows, heads_local, HEAD_SIZE
    )
    key_before_rotary = jnp.dot(full_attn, key_matrix, preferred_element_type=jnp.float32).reshape(
        sequence_rows, kv_local, HEAD_SIZE
    )
    query_rows = (
        apply_rotary(query_before_rotary, cosine_table, sine_values, 1.0)
        .astype(jnp.bfloat16)
        .reshape(sequence_rows, kv_local, query_groups, HEAD_SIZE)
    )
    keys_rot = apply_rotary(key_before_rotary, cosine_table, sine_values, 1.0).astype(jnp.bfloat16)
    value_inputs = (
        jnp.dot(full_attn, value_matrix, preferred_element_type=jnp.float32)
        .astype(jnp.bfloat16)
        .reshape(sequence_rows, kv_local, HEAD_SIZE)
    )
    row_start = 0
    row_stop = row_start + block_rows
    scores = block_scores(query_rows, keys_rot, seg_row, row_start, row_stop)
    peak_score = jnp.max(scores, axis=-1, keepdims=True)
    log_total = peak_score + jnp.log(jnp.sum(jnp.exp(scores - peak_score), axis=-1, keepdims=True))
    probs_blk = jnp.exp(scores - log_total)
    mixed_parts = jnp.einsum(
        "hgqk,khd->qhgd",
        probs_blk.astype(jnp.bfloat16),
        value_inputs,
        preferred_element_type=jnp.float32,
    ).astype(jnp.bfloat16)
    log_totals = [log_total]
    mixed_flat = mixed_parts.reshape(sequence_rows, heads_local * HEAD_SIZE)
    attn_out = lax.psum_scatter(
        jnp.dot(mixed_flat, attention_output_weight, preferred_element_type=jnp.float32),
        "tensor",
        scatter_dimension=0,
        tiled=True,
    )
    after_attn = rows_in + attn_out
    normed_ffn, unit_ffn, inverse_ffn = norm_forward(after_attn, gain_ffn)
    router_logits = jnp.dot(normed_ffn, w_router, preferred_element_type=jnp.float32)
    router_probs = jax.nn.softmax(router_logits, axis=-1)
    chosen_probs = jnp.take_along_axis(router_probs, routes, axis=1)
    picked_mask = (routes[:, :, None] == jnp.arange(experts_win)[None, None, :]).astype(jnp.float32)
    combine_bf = jnp.sum(chosen_probs[:, :, None] * picked_mask, axis=1).astype(jnp.bfloat16)
    full_ffn, full_combine = (
        lax.all_gather(normed_ffn, "tensor", axis=0, tiled=True),
        lax.all_gather(combine_bf, "tensor", axis=0, tiled=True),
    )
    combine_used = full_combine.astype(jnp.float32)
    combined = jnp.zeros((sequence_rows, width), jnp.float32)
    saved_parts = []
    for expert in range(experts_win):
        gate_pre = jnp.dot(full_ffn, w_gate[expert], preferred_element_type=jnp.float32)
        up_pre = jnp.dot(full_ffn, w_up[expert], preferred_element_type=jnp.float32)
        silu_val, slope_val = gate_parts(gate_pre)
        inner_act = (silu_val * up_pre).astype(jnp.bfloat16)
        expert_out = jnp.dot(inner_act, w_down[expert], preferred_element_type=jnp.float32)
        combined = combined + combine_used[:, expert : expert + 1] * expert_out
        saved_parts.append((up_pre, silu_val, slope_val, inner_act, expert_out))
    ffn_out = lax.psum_scatter(
        combined.astype(jnp.bfloat16), "tensor", scatter_dimension=0, tiled=True
    ).astype(jnp.float32)
    output = (after_attn + ffn_out).astype(jnp.bfloat16)
    grad_full = lax.all_gather(cotangent, "tensor", axis=0, tiled=True)
    grad_full32 = grad_full.astype(jnp.float32)
    partial_rows = jnp.zeros((sequence_rows, width), jnp.float32)
    grad_combine_list, grad_gate_list, grad_up_list, grad_down_list = ([], [], [], [])
    for expert in range(experts_win):
        up_pre, silu_val, slope_val, inner_act, expert_out = saved_parts[expert]
        grad_expert = (combine_used[:, expert : expert + 1] * grad_full32).astype(jnp.bfloat16)
        grad_combine_list.append(jnp.sum(grad_full32 * expert_out, axis=-1))
        grad_down_list.append(inner_rows(inner_act, grad_expert))
        grad_inner = outer_columns(grad_expert, w_down[expert])
        grad_gate_pre = (grad_inner * up_pre * slope_val).astype(jnp.bfloat16)
        grad_up_pre = (grad_inner * silu_val).astype(jnp.bfloat16)
        grad_gate_list.append(inner_rows(full_ffn, grad_gate_pre))
        grad_up_list.append(inner_rows(full_ffn, grad_up_pre))
        partial_rows = (
            partial_rows
            + outer_columns(grad_gate_pre, w_gate[expert])
            + outer_columns(grad_up_pre, w_up[expert])
        )
    grad_combine_part = jnp.stack(grad_combine_list, axis=1)
    grad_normed_part, grad_combine = (
        lax.psum_scatter(partial_rows, "tensor", scatter_dimension=0, tiled=True),
        lax.psum_scatter(grad_combine_part, "tensor", scatter_dimension=0, tiled=True),
    )
    grad_gate = jnp.stack(grad_gate_list)
    grad_up = jnp.stack(grad_up_list)
    grad_down = jnp.stack(grad_down_list)
    route_counts = jnp.sum(picked_mask, axis=1)
    grad_rprobs = jnp.concatenate(
        [
            grad_combine * route_counts,
            jnp.zeros((shard_rows, w_router.shape[1] - experts_win), jnp.float32),
        ],
        axis=1,
    )
    grad_logits = (
        router_probs * (grad_rprobs - jnp.sum(router_probs * grad_rprobs, axis=-1, keepdims=True))
    ).astype(jnp.bfloat16)
    grad_router = inner_rows(normed_ffn, grad_logits)
    grad_normed_ffn = grad_normed_part + outer_columns(grad_logits, w_router)
    grad_after, grad_gain_ffn = norm_backward(grad_normed_ffn, unit_ffn, inverse_ffn, gain_ffn)
    grad_after = grad_after + cotangent.astype(jnp.float32)
    full_grad_after = lax.all_gather(grad_after.astype(jnp.bfloat16), "tensor", axis=0, tiled=True)
    grad_w_out = inner_rows(mixed_flat, full_grad_after)
    mixed_gradient = (
        outer_columns(full_grad_after, attention_output_weight)
        .astype(jnp.bfloat16)
        .reshape(sequence_rows, kv_local, query_groups, HEAD_SIZE)
    )
    delta_rows = jnp.transpose(
        jnp.sum(mixed_gradient.astype(jnp.float32) * mixed_parts.astype(jnp.float32), axis=-1),
        (1, 2, 0),
    )[..., None]
    grad_keys = jnp.zeros((sequence_rows, kv_local, HEAD_SIZE), jnp.float32)
    value_gradients = jnp.zeros((sequence_rows, kv_local, HEAD_SIZE), jnp.float32)
    grad_query_parts = []
    for block_index, row_start in enumerate(range(0, sequence_rows, block_rows)):
        row_stop = row_start + block_rows
        scores = block_scores(query_rows, keys_rot, seg_row, row_start, row_stop)
        probs_blk = jnp.exp(scores - log_totals[block_index])
        value_gradients = value_gradients.at[:row_stop].add(
            jnp.einsum(
                "hgqk,qhgd->khd",
                probs_blk.astype(jnp.bfloat16),
                mixed_gradient,
                preferred_element_type=jnp.float32,
            )
        )
        grad_probs = jnp.einsum(
            "qhgd,khd->hgqk", mixed_gradient, value_inputs, preferred_element_type=jnp.float32
        )
        grad_scores = (probs_blk * (grad_probs - delta_rows) * scale_factor).astype(jnp.bfloat16)
        grad_query_parts.append(
            jnp.einsum("hgqk,khd->qhgd", grad_scores, keys_rot, preferred_element_type=jnp.float32)
        )
        grad_keys = grad_keys.at[:row_stop].add(
            jnp.einsum(
                "hgqk,qhgd->khd", grad_scores, query_rows, preferred_element_type=jnp.float32
            )
        )
    grad_query = grad_query_parts[0].reshape(sequence_rows, heads_local, HEAD_SIZE)
    grad_query_bf = (
        apply_rotary(grad_query, cosine_table, sine_values, -1.0)
        .astype(jnp.bfloat16)
        .reshape(sequence_rows, heads_local * HEAD_SIZE)
    )
    key_gradient_half = (
        apply_rotary(grad_keys, cosine_table, sine_values, -1.0)
        .astype(jnp.bfloat16)
        .reshape(sequence_rows, kv_local * HEAD_SIZE)
    )
    value_gradient_half = value_gradients.astype(jnp.bfloat16).reshape(
        sequence_rows, kv_local * HEAD_SIZE
    )
    grad_w_query = inner_rows(full_attn, grad_query_bf)
    grad_w_key = inner_rows(full_attn, key_gradient_half)
    grad_w_value = inner_rows(full_attn, value_gradient_half)
    grad_normed_attn = lax.psum_scatter(
        outer_columns(grad_query_bf, w_query)
        + outer_columns(key_gradient_half, key_matrix)
        + outer_columns(value_gradient_half, value_matrix),
        "tensor",
        scatter_dimension=0,
        tiled=True,
    )
    grad_in, grad_gain_attn = norm_backward(grad_normed_attn, unit_attn, inverse_attn, gain_attn)
    grad_in = grad_in + grad_after
    grad_router, grad_gain_attn, grad_gain_ffn = lax.psum(
        (grad_router, grad_gain_attn, grad_gain_ffn), ("dp", "tensor")
    )
    grad_w_query, grad_w_key, grad_w_value, grad_w_out, grad_gate, grad_up, grad_down = lax.psum(
        (grad_w_query, grad_w_key, grad_w_value, grad_w_out, grad_gate, grad_up, grad_down), "dp"
    )
    return (
        output,
        grad_in,
        grad_gain_attn,
        grad_w_query,
        grad_w_key,
        grad_w_value,
        grad_w_out,
        grad_gain_ffn,
        grad_router,
        grad_gate,
        grad_up,
        grad_down,
    )


def solution(mesh):
    return jax.shard_map(
        on_device,
        mesh=mesh,
        in_specs=(
            P(("dp", "tensor"), None),
            P(("dp", "tensor"), None),
            P("dp", None),
            P(("dp", "tensor"), None),
            P(),
            P(None, "tensor"),
            P(None, "tensor"),
            P(None, "tensor"),
            P("tensor", None),
            P(),
            P(),
            P(None, None, "tensor"),
            P(None, None, "tensor"),
            P(None, "tensor", None),
        ),
        out_specs=(
            P(("dp", "tensor"), None),
            P(("dp", "tensor"), None),
            P(),
            P(None, "tensor"),
            P(None, "tensor"),
            P(None, "tensor"),
            P("tensor", None),
            P(),
            P(),
            P(None, None, "tensor"),
            P(None, None, "tensor"),
            P(None, "tensor", None),
        ),
        check_vma=False,
    )
```

profile of v0, /device:TPU:0, one launch (start us, length us, event | category | flops | bytes accessed | tf_op | source)
XLA Modules:
  0.0 624.9 jit_solution(6385940482338524019)
XLA Ops:
  7.3 1.2 fusion.21
  8.4 1.8 fusion.15
  11.3 1.0 fusion.10
  12.2 17.6 %all-gather.5.cloned.1.call-done = bf16[512,1024]{1,0:T(8,128)(2,1)} async-done(((bf16[128,1024]{1,0:T(8,128)(2,1)}), bf16[512,1024]{1,0:T(8,128)(2,1)}) %all-gather.5.cloned.1.call-update) | async-done | bytes 1048592 | tf_op jit(solution)/shard_map/all_gather | solution.py:103
  29.8 1.8 fusion.83
  35.3 1.3 convolution_convert_fusion.1
  36.6 1.8 fusion.85
  38.5 31.2 %reduce-scatter.8.cloned.1.call-done = f32[128,1024]{1,0:T(8,128)} async-done(((f32[512,1024]{1,0:T(8,128)}), f32[128,1024]{1,0:T(8,128)}) %reduce-scatter.8.cloned.1.call-update) | async-done | bytes 524304 | tf_op jit(solution)/shard_map/reduce_scatter | solution.py:135
  69.7 1.2 multiply_reduce_fusion.3
  72.6 1.2 fusion.82
  73.9 7.0 %gather_fusion = f32[1024]{0:T(1024)S(1)} fusion(f32[128,32]{0,1:T(8,128)S(1)} %fusion.68, s32[1024]{0:T(1024)S(1)} %reshape.279), kind=kCustom, calls=%fused_computation | custom fusion | bytes 16384 | tf_op jit(solution)/shard_map/jit(take_along_axis)/gather | solution.py:145
  82.6 5.1 all_gather.16
  88.7 2.4 fusion.32
  91.0 1.7 fusion.36
  92.7 14.1 %all-gather.9.cloned.1.call-done = bf16[512,1024]{1,0:T(8,128)(2,1)} async-done(((bf16[128,1024]{1,0:T(8,128)(2,1)}), bf16[512,1024]{1,0:T(8,128)(2,1)}) %all-gather.9.cloned.1.call-update) | async-done | bytes 1048592 | tf_op jit(solution)/shard_map/all_gather | solution.py:167
  106.8 2.6 multiply_convert_fusion.1
  112.1 1.2 multiply_convert_fusion.3
  113.3 1.7 fusion.7
  116.0 1.5 fusion.34
  118.5 1.8 add_add_fusion.1
  120.5 15.6 %reduce-scatter.16.cloned.1.call-done = f32[128,2]{1,0:T(8,128)} async-done(((f32[512,2]{1,0:T(8,128)}), f32[128,2]{1,0:T(8,128)}) %reduce-scatter.16.cloned.1.call-update) | async-done | bytes 1040
  137.1 32.6 %reduce-scatter.12.cloned.1.call-done = f32[128,1024]{1,0:T(8,128)} async-done(((f32[512,1024]{1,0:T(8,128)}), f32[128,1024]{1,0:T(8,128)}) %reduce-scatter.12.cloned.1.call-update) | async-done | bytes 524304 | tf_op jit(solution)/shard_map/reduce_scatter | solution.py:188
  169.7 2.1 multiply_reduce_fusion
  172.6 1.9 fusion.80
  174.5 16.8 %all-gather.11.cloned.1.call-done = bf16[512,1024]{1,0:T(8,128)(2,1)} async-done(((bf16[128,1024]{1,0:T(8,128)(2,1)}), bf16[512,1024]{1,0:T(8,128)(2,1)}) %all-gather.11.cloned.1.call-update) | async-done | bytes 1048592 | tf_op jit(solution)/shard_map/all_gather | solution.py:209
  191.3 1.8 multiply_reduce_fusion.1
  193.1 3.5 fusion.9
  196.7 1.6 fusion.2
  201.9 1.8 add_add_fusion
  204.6 1.7 convolution_bitcast_fusion.1
  206.3 1.4 convolution_bitcast_fusion
  207.7 1.1 pad_maximum_fusion.2
  210.8 1.5 pad_maximum_fusion
  213.1 2.7 fusion.91
  215.8 1.3 fusion.89
  217.1 1.5 fusion.88
  218.5 1.3 fusion.90
  219.9 15.2 %reduce-scatter.14.cloned.1.call-done = f32[128,1024]{1,0:T(8,128)} async-done(((f32[512,1024]{1,0:T(8,128)}), f32[128,1024]{1,0:T(8,128)}) %reduce-scatter.14.cloned.1.call-update) | async-done | bytes 524304 | tf_op jit(solution)/shard_map/reduce_scatter | solution.py:264
  235.1 1.3 fusion.20
  236.4 39.4 %all-reduce.1 = (f32[1024]{0:T(1024)}, f32[1024]{0:T(1024)}) all-reduce(f32[1024]{0:T(1024)S(1)} %get-tuple-element.56, f32[1024]{0:T(1024)S(1)} %copy-done.68), channel_id=1, replica_groups=mesh['dp'=8,'tensor'=4] {'dp','tensor'}, use_global_device_ids=true, to_apply=%region_20.21 | all-reduce | flops 2048 | bytes 16384 | tf_op jit(solution)/shard_map/psum | solution.py:274
  275.9 2.2 fusion.19
  278.1 115.5 %all-reduce.6.cloned.1.call-done = f32[1024,32]{0,1:T(8,128)} async-done(((f32[1024,32]{0,1:T(8,128)}), f32[1024,32]{0,1:T(8,128)}) %all-reduce.6.cloned.1.call-update) | async-done | bytes 131088 | tf_op jit(solution)/shard_map/psum | solution.py:274
  393.6 216.3 %all-reduce.8.cloned.1.call-done = (f32[1024,256]{1,0:T(8,128)}, f32[1024,128]{1,0:T(8,128)}, f32[1024,128]{1,0:T(8,128)}, f32[256,1024]{1,0:T(8,128)}, f32[2,10...) async-done(((f32[1024,256]{1,0:T(8,128)}, f32[1024,128]{1,0:T(8,128)}, f32[1024,128]{1,0:T(8,128)}, f32[256,1024]{1,0:T(8,128)}, ...) | async-done | bytes 6291472 | tf_op jit(solution)/shard_map/psum | solution.py:277
  609.8 2.4 copy.86
  613.8 1.0 copy.89
  615.5 1.0 copy.91
  616.5 1.0 copy.92
  617.4 1.0 copy.93
  (229 shorter events, 24.8 us)
Async XLA Ops:
  7.2 29.4 %copy-start = (bf16[256,1024]{1,0:T(8,128)(2,1)S(1)}, bf16[256,1024]{1,0:T(8,128)(2,1)}, u32[]{:S(2)}) copy-start(bf16[256,1024]{1,0:T(8,128)(2,1)} %param.30) | copy-start | bytes 1572868
  7.2 24.5 %copy-start.20 = (bf16[1024,256]{1,0:T(8,128)(2,1)S(1)}, bf16[1024,256]{1,0:T(8,128)(2,1)}, u32[]{:S(2)}) copy-start(bf16[1024,256]{1,0:T(8,128)(2,1)} %param.27) | copy-start | bytes 1572868
  7.2 22.6 %all-gather.5.cloned.1.call-start = ((), (), s32[]{:S(2)}) async-start(), calls=%async_computation.5 | async-start | bytes 1310720 | tf_op jit(solution)/shard_map/all_gather | solution.py:103
  8.4 2.8 copy-start.73
  10.3 59.5 %reduce-scatter.8.cloned.1.call-start = ((), (), s32[]{:S(2)}) async-start(), calls=%async_computation.6 | async-start | bytes 2621440 | tf_op jit(solution)/shard_map/reduce_scatter | solution.py:135
  12.2 22.7 %copy-start.22 = (pred[512,512]{0,1:T(8,128)(4,1)}, pred[512,512]{0,1:T(8,128)(4,1)S(1)}, u32[]{:S(2)}) copy-start(pred[512,512]{0,1:T(8,128)(4,1)S(1)} %fusion.10) | copy-start | bytes 786436
  36.6 33.2 %copy-start.5 = (bf16[128,1024]{1,0:T(8,128)(2,1)S(1)}, bf16[128,1024]{1,0:T(8,128)(2,1)}, u32[]{:S(2)}) copy-start(bf16[128,1024]{1,0:T(8,128)(2,1)} %param.22) | copy-start | bytes 786436
  38.4 32.5 %copy-start.60 = (f32[1024]{0:T(1024)S(1)}, f32[1024]{0:T(1024)}, u32[]{:S(2)}) copy-start(f32[1024]{0:T(1024)} %param.31) | copy-start | bytes 12292
  38.4 34.0 %copy-start.63 = (s32[128,8]{0,1:T(8,128)S(1)}, s32[128,8]{0,1:T(8,128)}, u32[]{:S(2)}) copy-start(s32[128,8]{0,1:T(8,128)} %param.25) | copy-start | bytes 12292
  38.4 34.2 %copy-start.52 = (bf16[1024,32]{0,1:T(8,128)(2,1)S(1)}, bf16[1024,32]{0,1:T(8,128)(2,1)}, u32[]{:S(2)}) copy-start(bf16[1024,32]{0,1:T(8,128)(2,1)} %param.32) | copy-start | bytes 196612
  38.4 50.2 %all-gather.7.cloned.1.call-start = ((), (), s32[]{:S(2)}) async-start(), calls=%async_computation.7 | async-start | bytes 1310720 | tf_op jit(solution)/shard_map/all_gather | solution.py:149
  70.9 100.8 %copy-start.69 = (f32[128]{0:T(128)}, f32[128]{0:T(128)S(1)}, u32[]{:S(2)}) copy-start(f32[128]{0:T(128)S(1)} %add_rsqrt_fusion) | copy-start | bytes 1540
  71.8 35.0 %all-gather.9.cloned.1.call-start = ((), (), s32[]{:S(2)}) async-start(), calls=%async_computation.9 | async-start | bytes 1310720 | tf_op jit(solution)/shard_map/all_gather | solution.py:167
  72.4 63.7 %reduce-scatter.16.cloned.1.call-start = ((), (), s32[]{:S(2)}) async-start(), calls=%async_computation.14 | async-start | bytes 327680
  73.9 14.8 %copy-start.17 = (bf16[2,1024,128]{2,1,0:T(8,128)(2,1)S(1)}, bf16[2,1024,128]{2,1,0:T(8,128)(2,1)}, u32[]{:S(2)}) copy-start(bf16[2,1024,128]{2,1,0:T(8,128)(2,1)} %param.34) | copy-start | bytes 1572868
  73.9 17.2 %copy-start.14 = (bf16[2,1024,128]{2,1,0:T(8,128)(2,1)S(1)}, bf16[2,1024,128]{2,1,0:T(8,128)(2,1)}, u32[]{:S(2)}) copy-start(bf16[2,1024,128]{2,1,0:T(8,128)(2,1)} %param.33) | copy-start | bytes 1572868
  87.7 25.6 %copy-start.64 = (f32[512,1]{0,1:T(1,128)}, f32[512,1]{0,1:T(1,128)S(1)}, u32[]{:S(2)}) copy-start(f32[512,1]{0,1:T(1,128)S(1)} %get-tuple-element.92) | copy-start | bytes 6148
  87.7 25.6 %copy-start.65 = (f32[512,1]{0,1:T(1,128)}, f32[512,1]{0,1:T(1,128)S(1)}, u32[]{:S(2)}) copy-start(f32[512,1]{0,1:T(1,128)S(1)} %get-tuple-element.91) | copy-start | bytes 6148
  106.8 3.3 copy-start.36
  115.9 53.8 %reduce-scatter.12.cloned.1.call-start = ((), (), s32[]{:S(2)}) async-start(), calls=%async_computation.10 | async-start | bytes 2621440 | tf_op jit(solution)/shard_map/reduce_scatter | solution.py:188
  120.3 71.0 %all-gather.11.cloned.1.call-start = ((), (), s32[]{:S(2)}) async-start(), calls=%async_computation.11 | async-start | bytes 1310720 | tf_op jit(solution)/shard_map/all_gather | solution.py:209
  137.0 56.1 %copy-start.66 = (f32[128,2]{0,1:T(2,128)}, f32[128,2]{0,1:T(2,128)S(1)}, u32[]{:S(2)}) copy-start(f32[128,2]{0,1:T(2,128)S(1)} %mul.511) | copy-start | bytes 3076
  137.1 56.0 %copy-start.71 = (f32[128]{0:T(128)}, f32[128]{0:T(128)S(1)}, u32[]{:S(2)}) copy-start(f32[128]{0:T(128)S(1)} %fusion.65) | copy-start | bytes 1540
  171.8 24.9 %copy-start.75 = (f32[128]{0:T(128)}, f32[128]{0:T(128)S(1)}, u32[]{:S(2)}) copy-start(f32[128]{0:T(128)S(1)} %broadcast_multiply_fusion.2) | copy-start | bytes 1540
  174.4 60.6 %reduce-scatter.14.cloned.1.call-start = ((), (), s32[]{:S(2)}) async-start(), calls=%async_computation.12 | async-start | bytes 2621440 | tf_op jit(solution)/shard_map/reduce_scatter | solution.py:264
  193.1 3.6 copy-start.9
  193.1 3.6 copy-start.59
  196.7 3.2 copy-start.50
  203.8 72.0 %reduce-scatter.10.cloned.1.call-start = ((), (), s32[]{:S(2)}) async-start(), calls=%async_computation.8 | async-start | bytes 1310720 | tf_op jit(solution)/shard_map/reduce_scatter | solution.py:163
  204.5 189.1 %all-reduce.6.cloned.1.call-start = ((), (), s32[]{:S(2)}) async-start(), calls=%async_computation.13 | async-start | bytes 262144 | tf_op jit(solution)/shard_map/psum | solution.py:274
  206.3 2.5 copy-start.48
  213.1 4.0 copy-start.12
  213.1 396.7 %all-reduce.8.cloned.1.call-start = ((), (), s32[]{:S(2)}) async-start(), calls=%async_computation.15 | async-start | bytes 12582912 | tf_op jit(solution)/shard_map/psum | solution.py:277
  215.8 2.7 copy-start.51
  219.8 15.3 %copy-start.62 = (f32[1024]{0:T(1024)S(1)}, f32[1024]{0:T(1024)}, u32[]{:S(2)}) copy-start(f32[1024]{0:T(1024)} %param.26) | copy-start | bytes 12292
  219.8 15.3 %copy-start.74 = (f32[128]{0:T(128)S(1)}, f32[128]{0:T(128)}, u32[]{:S(2)}) copy-start(f32[128]{0:T(128)} %copy-done.73) | copy-start | bytes 1540
  219.8 16.6 %copy-start.68 = (f32[1024]{0:T(1024)S(1)}, f32[1024]{0:T(1024)}, u32[]{:S(2)}) copy-start(f32[1024]{0:T(1024)} %get-tuple-element.52) | copy-start | bytes 12292
  219.8 56.0 %copy-start.7 = (f32[128,1024]{1,0:T(8,128)S(1)}, f32[128,1024]{1,0:T(8,128)}, u32[]{:S(2)}) copy-start(f32[128,1024]{1,0:T(8,128)} %copy-done.6) | copy-start | bytes 1572868
  219.8 56.0 %copy-start.13 = (bf16[128,1024]{1,0:T(8,128)(2,1)S(1)}, bf16[128,1024]{1,0:T(8,128)(2,1)}, u32[]{:S(2)}) copy-start(bf16[128,1024]{1,0:T(8,128)(2,1)} %param.23) | copy-start | bytes 786436
  219.8 56.0 %copy-start.61 = (f32[1024]{0:T(1024)S(1)}, f32[1024]{0:T(1024)}, u32[]{:S(2)}) copy-start(f32[1024]{0:T(1024)} %param.31) | copy-start | bytes 12292
  219.8 56.0 %copy-start.70 = (f32[128]{0:T(128)S(1)}, f32[128]{0:T(128)}, u32[]{:S(2)}) copy-start(f32[128]{0:T(128)} %copy-done.69) | copy-start | bytes 1540
  219.9 56.0 %copy-start.76 = (f32[128]{0:T(128)S(1)}, f32[128]{0:T(128)}, u32[]{:S(2)}) copy-start(f32[128]{0:T(128)} %copy-done.75) | copy-start | bytes 1540
  609.8 2.4 copy-start.42
  609.8 3.2 copy-start.41
  609.8 4.0 copy-start.27
  612.2 2.6 copy-start.57
  612.2 3.2 copy-start.26
  613.8 2.6 copy-start.25
  (40 other events, 56.7 us)
Sparse Core Ops, SparseCore 0:
  10.4 19.4 all-gather.4
  38.5 31.1 reduce-scatter.7
  71.9 16.7 all-gather.6
  90.1 16.6 all-gather.8
  116.0 20.0 reduce-scatter.15
  138.5 31.1 reduce-scatter.11
  174.5 16.6 all-gather.10
  203.9 31.1 reduce-scatter.13
  238.2 24.8 reduce-scatter.9
  269.0 124.5 all-reduce.5
  400.0 209.8 all-reduce.7
where the time goes:
time: 626 us; the launch traced here: 625 us
  waiting for transfers between devices  477 us (76%)
  matrix products  48.4 us (8%)
  blocking collectives  44.6 us (7%)
  local copies, waits for them, and re-layouts  23.2 us (4%)
  other arithmetic  16.2 us (3%)
  between operations  14.8 us (2%)
    psum x1, waiting for transfers between devices, on_device(): lax.psum((grad_w_query, grad_w_key, grad_w_value, grad_w_out, grad_gate,...  216 us
    psum x1, waiting for transfers between devices, on_device(): lax.psum((grad_router, grad_gain_attn, grad_gain_ffn), ('dp', 'tensor'))  115 us
    psum x1, blocking collectives, on_device(): lax.psum((grad_router, grad_gain_attn, grad_gain_ffn), ('dp', 'tensor'))  39.4 us
    reduce_scatter x1, waiting for transfers between devices, on_device(): lax.psum_scatter(partial_rows, 'tensor', scatter_dimension=0, tiled=True)  32.6 us
    reduce_scatter x1, waiting for transfers between devices, on_device(): lax.psum_scatter(jnp.dot(mixed_flat, attention_output_weight, preferred_e...  31.2 us
    all_gather x1, waiting for transfers between devices, on_device(): full_attn = lax.all_gather(attention_normed, 'tensor', axis=0, tiled=True)  17.6 us
    unnamed x12, waiting for transfers between devices  16.9 us
    all_gather x1, waiting for transfers between devices, on_device(): lax.all_gather(grad_after.astype(jnp.bfloat16), 'tensor', axis=0, tiled=T...  16.8 us
  transfers between devices with their start and end apart: 11, of which 10 were waited for; matrix products, arithmetic and copies ran while one was open for 6% of the time, Pallas kernels for 0%

commit v1 on v0

--- a/solution.py
+++ b/solution.py
@@ -59,6 +59,17 @@
 def gate_parts(gate_pre):
     sig_vals = jax.nn.sigmoid(gate_pre)
     return (gate_pre * sig_vals, sig_vals * (1.0 + gate_pre * (1.0 - sig_vals)))
+
+
+def beside(left, right):
+    pad = jnp.zeros((right.shape[0], 128 - right.shape[1]), left.dtype)
+    return jnp.concatenate([left, right.astype(left.dtype), pad], axis=1)
+
+
+def scatter_sum(part):
+    return lax.psum_scatter(
+        part.astype(jnp.bfloat16), "tensor", scatter_dimension=0, tiled=True
+    ).astype(jnp.float32)
 
 
 def block_scores(query_block, keys_part, seg_row, row_start, row_stop):
@@ -100,7 +111,11 @@
     cosine_table, sine_values = rotary_tables(sequence_rows)
     rows_in = hidden_in.astype(jnp.float32)
     attention_normed, unit_attn, inverse_attn = norm_forward(rows_in, gain_attn)
-    full_attn = lax.all_gather(attention_normed, "tensor", axis=0, tiled=True)
+    gathered = lax.all_gather(
+        jnp.concatenate([attention_normed, cotangent], axis=1), "tensor", axis=0, tiled=True
+    )
+    full_attn = gathered[:, :width]
+    grad_full = gathered[:, width:]
     query_before_rotary = jnp.dot(full_attn, w_query, preferred_element_type=jnp.float32).reshape(
         sequence_rows, heads_local, HEAD_SIZE
     )
@@ -132,23 +147,19 @@
     ).astype(jnp.bfloat16)
     log_totals = [log_total]
     mixed_flat = mixed_parts.reshape(sequence_rows, heads_local * HEAD_SIZE)
-    attn_out = lax.psum_scatter(
-        jnp.dot(mixed_flat, attention_output_weight, preferred_element_type=jnp.float32),
-        "tensor",
-        scatter_dimension=0,
-        tiled=True,
+    attn_out = scatter_sum(
+        jnp.dot(mixed_flat, attention_output_weight, preferred_element_type=jnp.float32)
     )
     after_attn = rows_in + attn_out
     normed_ffn, unit_ffn, inverse_ffn = norm_forward(after_attn, gain_ffn)
     router_logits = jnp.dot(normed_ffn, w_router, preferred_element_type=jnp.float32)
     router_probs = jax.nn.softmax(router_logits, axis=-1)
-    chosen_probs = jnp.take_along_axis(router_probs, routes, axis=1)
     picked_mask = (routes[:, :, None] == jnp.arange(experts_win)[None, None, :]).astype(jnp.float32)
-    combine_bf = jnp.sum(chosen_probs[:, :, None] * picked_mask, axis=1).astype(jnp.bfloat16)
-    full_ffn, full_combine = (
-        lax.all_gather(normed_ffn, "tensor", axis=0, tiled=True),
-        lax.all_gather(combine_bf, "tensor", axis=0, tiled=True),
-    )
+    route_counts = jnp.sum(picked_mask, axis=1)
+    combine_bf = (router_probs[:, :experts_win] * route_counts).astype(jnp.bfloat16)
+    gathered_ffn = lax.all_gather(beside(normed_ffn, combine_bf), "tensor", axis=0, tiled=True)
+    full_ffn = gathered_ffn[:, :width]
+    full_combine = gathered_ffn[:, width : width + experts_win]
     combine_used = full_combine.astype(jnp.float32)
     combined = jnp.zeros((sequence_rows, width), jnp.float32)
     saved_parts = []
@@ -160,11 +171,7 @@
         expert_out = jnp.dot(inner_act, w_down[expert], preferred_element_type=jnp.float32)
         combined = combined + combine_used[:, expert : expert + 1] * expert_out
         saved_parts.append((up_pre, silu_val, slope_val, inner_act, expert_out))
-    ffn_out = lax.psum_scatter(
-        combined.astype(jnp.bfloat16), "tensor", scatter_dimension=0, tiled=True
-    ).astype(jnp.float32)
-    output = (after_attn + ffn_out).astype(jnp.bfloat16)
-    grad_full = lax.all_gather(cotangent, "tensor", axis=0, tiled=True)
+    combined = combined.astype(jnp.bfloat16)
     grad_full32 = grad_full.astype(jnp.float32)
     partial_rows = jnp.zeros((sequence_rows, width), jnp.float32)
     grad_combine_list, grad_gate_list, grad_up_list, grad_down_list = ([], [], [], [])
@@ -176,22 +183,18 @@
         grad_inner = outer_columns(grad_expert, w_down[expert])
         grad_gate_pre = (grad_inner * up_pre * slope_val).astype(jnp.bfloat16)
         grad_up_pre = (grad_inner * silu_val).astype(jnp.bfloat16)
-        grad_gate_list.append(inner_rows(full_ffn, grad_gate_pre))
-        grad_up_list.append(inner_rows(full_ffn, grad_up_pre))
+        grad_gate_list.append(grad_gate_pre)
+        grad_up_list.append(grad_up_pre)
         partial_rows = (
             partial_rows
             + outer_columns(grad_gate_pre, w_gate[expert])
             + outer_columns(grad_up_pre, w_up[expert])
         )
     grad_combine_part = jnp.stack(grad_combine_list, axis=1)
-    grad_normed_part, grad_combine = (
-        lax.psum_scatter(partial_rows, "tensor", scatter_dimension=0, tiled=True),
-        lax.psum_scatter(grad_combine_part, "tensor", scatter_dimension=0, tiled=True),
-    )
-    grad_gate = jnp.stack(grad_gate_list)
-    grad_up = jnp.stack(grad_up_list)
-    grad_down = jnp.stack(grad_down_list)
-    route_counts = jnp.sum(picked_mask, axis=1)
+    scattered = scatter_sum(beside(partial_rows.astype(jnp.bfloat16), grad_combine_part))
+    grad_normed_part = scattered[:, :width]
+    grad_combine = scattered[:, width : width + experts_win]
+    grad_down = jnp.concatenate(grad_down_list, axis=0)
     grad_rprobs = jnp.concatenate(
         [
             grad_combine * route_counts,
@@ -202,11 +205,17 @@
     grad_logits = (
         router_probs * (grad_rprobs - jnp.sum(router_probs * grad_rprobs, axis=-1, keepdims=True))
     ).astype(jnp.bfloat16)
-    grad_router = inner_rows(normed_ffn, grad_logits)
     grad_normed_ffn = grad_normed_part + outer_columns(grad_logits, w_router)
     grad_after, grad_gain_ffn = norm_backward(grad_normed_ffn, unit_ffn, inverse_ffn, gain_ffn)
     grad_after = grad_after + cotangent.astype(jnp.float32)
-    full_grad_after = lax.all_gather(grad_after.astype(jnp.bfloat16), "tensor", axis=0, tiled=True)
+    gathered_after = lax.all_gather(
+        beside(grad_after.astype(jnp.bfloat16), grad_logits), "tensor", axis=0, tiled=True
+    )
+    full_grad_after = gathered_after[:, :width]
+    full_logits = gathered_after[:, width:]
+    ffn_sums = inner_rows(
+        full_ffn, jnp.concatenate(grad_gate_list + grad_up_list + [full_logits], axis=1)
+    ).astype(jnp.bfloat16)
     grad_w_out = inner_rows(mixed_flat, full_grad_after)
     mixed_gradient = (
         outer_columns(full_grad_after, attention_output_weight)
@@ -258,25 +267,44 @@
     value_gradient_half = value_gradients.astype(jnp.bfloat16).reshape(
         sequence_rows, kv_local * HEAD_SIZE
     )
-    grad_w_query = inner_rows(full_attn, grad_query_bf)
-    grad_w_key = inner_rows(full_attn, key_gradient_half)
-    grad_w_value = inner_rows(full_attn, value_gradient_half)
-    grad_normed_attn = lax.psum_scatter(
+    attn_sums = inner_rows(
+        full_attn,
+        jnp.concatenate([grad_query_bf, key_gradient_half, value_gradient_half], axis=1),
+    ).astype(jnp.bfloat16)
+    row_sums = jnp.concatenate([grad_down, grad_w_out], axis=0).astype(jnp.bfloat16)
+    grad_normed_attn = scatter_sum(
         outer_columns(grad_query_bf, w_query)
         + outer_columns(key_gradient_half, key_matrix)
-        + outer_columns(value_gradient_half, value_matrix),
-        "tensor",
-        scatter_dimension=0,
-        tiled=True,
-    )
+        + outer_columns(value_gradient_half, value_matrix)
+    )
+    grad_normed_attn, combined = lax.optimization_barrier((grad_normed_attn, combined))
+    output = (after_attn + scatter_sum(combined)).astype(jnp.bfloat16)
     grad_in, grad_gain_attn = norm_backward(grad_normed_attn, unit_attn, inverse_attn, gain_attn)
     grad_in = grad_in + grad_after
-    grad_router, grad_gain_attn, grad_gain_ffn = lax.psum(
-        (grad_router, grad_gain_attn, grad_gain_ffn), ("dp", "tensor")
-    )
-    grad_w_query, grad_w_key, grad_w_value, grad_w_out, grad_gate, grad_up, grad_down = lax.psum(
-        (grad_w_query, grad_w_key, grad_w_value, grad_w_out, grad_gate, grad_up, grad_down), "dp"
-    )
+    gains = jnp.concatenate([grad_gain_ffn, grad_gain_attn]).reshape(-1, 128)
+    gains = lax.psum(gains, ("dp", "tensor"))
+    ffn_sums, row_sums, attn_sums = lax.psum((ffn_sums, row_sums, attn_sums), "dp")
+    ffn_sums = ffn_sums.astype(jnp.float32)
+    row_sums = row_sums.astype(jnp.float32)
+    attn_sums = attn_sums.astype(jnp.float32)
+    hidden = w_gate.shape[2]
+    grad_gate = jnp.stack([ffn_sums[:, e * hidden : (e + 1) * hidden] for e in range(experts_win)])
+    grad_up = jnp.stack(
+        [ffn_sums[:, e * hidden : (e + 1) * hidden] for e in range(experts_win, 2 * experts_win)]
+    )
+    grad_router = ffn_sums[:, 2 * experts_win * hidden :]
+    query_cols = w_query.shape[1]
+    key_cols = key_matrix.shape[1]
+    grad_w_query = attn_sums[:, :query_cols]
+    grad_w_key = attn_sums[:, query_cols : query_cols + key_cols]
+    grad_w_value = attn_sums[:, query_cols + key_cols :]
+    down_rows = grad_down.shape[0]
+    grad_down = row_sums[:down_rows]
+    grad_w_out = row_sums[down_rows:]
+    gains = gains.reshape(2, width)
+    grad_gain_ffn, grad_gain_attn = gains[0], gains[1]
+    grad_router = grad_router[:, : w_router.shape[1]]
+    grad_down = grad_down.reshape(w_down.shape)
     return (
         output,
         grad_in,

time: 626 us -> 370 us (0.59)
  waiting for transfers between devices: 477 us -> 238 us
  matrix products: 48.4 us -> 33.2 us
    psum x2 -> x1, waiting for transfers between devices: 332 us -> 97.5 us  [on_device(): lax.psum((ffn_sums, row_sums, attn_sums), 'dp')]
    unnamed x12 -> x8, waiting for transfers between devices: 16.9 us -> 0.13 us
    all_gather x4 -> x3, waiting for transfers between devices: 49.4 us -> 59.9 us  [the longest x1 24.8 us: on_device(): lax.all_gather(jnp.concatenate([attention_normed, cotangent], axis=1), 't...]
    gather x5 -> x0, local copies, waits for them, and re-layouts: 8.81 us -> none  [on_device(): chosen_probs = jnp.take_along_axis(router_probs, routes, axis=1)]
    unnamed x164 -> x127, local copies, waits for them, and re-layouts: 14.4 us -> 6.04 us
    dot_general x11, matrix products: 14.6 us -> 7.19 us  [outer_columns(): lax.dot_general(left_op, right_op, (((1,), (1,)), ((), ())), preferred_el...]
  transfers between devices with their start and end apart: 11 -> 8, of which waited for: 10 -> 8; matrix products, arithmetic and copies ran while one was open for 6% -> 6% of each run, Pallas kernels for 0% -> 0%
where the time goes in v1:
time: 370 us; the launch traced here: 369 us
  waiting for transfers between devices  238 us (64%)
  blocking collectives  42.8 us (12%)
  matrix products  33.2 us (9%)
  local copies, waits for them, and re-layouts  19.7 us (5%)
  other arithmetic  18.8 us (5%)
  between operations  15.1 us (4%)
    psum x1, waiting for transfers between devices, on_device(): lax.psum((ffn_sums, row_sums, attn_sums), 'dp')  97.5 us
    reduce_scatter x4, waiting for transfers between devices, scatter_sum(): lax.psum_scatter(part.astype(jnp.bfloat16), 'tensor', scatter_dimension=0...  80.7 us
    psum x1, blocking collectives, on_device(): gains = lax.psum(gains, ('dp', 'tensor'))  42.8 us
    all_gather x1, waiting for transfers between devices, on_device(): lax.all_gather(jnp.concatenate([attention_normed, cotangent], axis=1), 't...  24.8 us
    all_gather x1, waiting for transfers between devices, on_device(): lax.all_gather(beside(grad_after.astype(jnp.bfloat16), grad_logits), 'ten...  17.5 us
    all_gather x1, waiting for transfers between devices, on_device(): lax.all_gather(beside(normed_ffn, combine_bf), 'tensor', axis=0, tiled=True)  17.5 us
    dot_general x5, matrix products, inner_rows(): lax.dot_general(left_op, right_op, (((0,), (0,)), ((), ())), preferred_el...  7.61 us
  transfers between devices with their start and end apart: 8, of which 8 were waited for; matrix products, arithmetic and copies ran while one was open for 6% of the time, Pallas kernels for 0%

profile of v1, /device:TPU:0, one launch (start us, length us, event | category | flops | bytes accessed | tf_op | source)
XLA Modules:
  0.0 368.5 jit_solution(15019208797739377973)
XLA Ops:
  7.3 1.2 fusion.38
  8.4 1.1 fusion.32
  9.5 1.8 pad_maximum_fusion.3
  11.9 24.8 %all-gather.4.cloned.1.call-done = bf16[512,2048]{1,0:T(8,128)(2,1)} async-done(((bf16[128,2048]{1,0:T(8,128)(2,1)}), bf16[512,2048]{1,0:T(8,128)(2,1)}) %all-gather.4.cloned.1.call-update) | async-done | bytes 2097168 | tf_op jit(solution)/shard_map/all_gather | solution.py:114
  36.8 1.9 fusion.18
  39.3 0.9 fusion.4
  40.3 0.9 exponential_reduce_fusion
  42.3 1.3 convolution_convert_fusion.7
  44.2 1.4 convolution_convert_fusion.1
  45.8 24.9 %reduce-scatter.5.cloned.1.call-done = bf16[128,1024]{1,0:T(8,128)(2,1)} async-done(((bf16[512,1024]{1,0:T(8,128)(2,1)}), bf16[128,1024]{1,0:T(8,128)(2,1)}) %reduce-scatter.5.cloned.1.call-update) | async-done | bytes 262160 | tf_op jit(solution)/shard_map/reduce_scatter | solution.py:70
  70.7 1.1 multiply_reduce_fusion.3
  72.3 1.1 multiply_convert_fusion
  74.3 0.8 concatenate.64
  75.2 17.5 %all-gather.6.cloned.1.call-done = bf16[512,1152]{1,0:T(8,128)(2,1)} async-done(((bf16[128,1152]{1,0:T(8,128)(2,1)}), bf16[512,1152]{1,0:T(8,128)(2,1)}) %all-gather.6.cloned.1.call-update) | async-done | bytes 1179664 | tf_op jit(solution)/shard_map/all_gather | solution.py:160
  92.7 1.0 slice_convert_fusion
  94.1 1.8 fusion.30
  100.7 1.8 fusion.8
  102.4 0.8 stack.36
  103.2 0.8 stack.37
  105.2 2.9 concatenate.65
  108.4 25.5 %reduce-scatter.7.cloned.1.call-done = bf16[128,1152]{1,0:T(8,128)(2,1)} async-done(((bf16[512,1152]{1,0:T(8,128)(2,1)}), bf16[128,1152]{1,0:T(8,128)(2,1)}) %reduce-scatter.7.cloned.1.call-update) | async-done | bytes 294928 | tf_op jit(solution)/shard_map/reduce_scatter | solution.py:70
  133.9 1.0 convert_element_type.244
  136.5 0.8 concatenate.67
  137.3 17.5 %all-gather.8.cloned.1.call-done = bf16[512,1152]{1,0:T(8,128)(2,1)} async-done(((bf16[128,1152]{1,0:T(8,128)(2,1)}), bf16[512,1152]{1,0:T(8,128)(2,1)}) %all-gather.8.cloned.1.call-update) | async-done | bytes 1179664 | tf_op jit(solution)/shard_map/all_gather | solution.py:211
  154.9 1.7 multiply_reduce_fusion.1
  156.6 3.5 fusion.9
  160.2 1.6 fusion.2
  161.9 0.7 convolution_bitcast_fusion.1
  164.3 1.5 add_convert_fusion.1
  165.9 1.7 convolution_convert_fusion.4
  167.7 1.6 convolution_convert_fusion.5
  169.8 1.0 pad_maximum_fusion
  170.9 0.7 copy-done.24
  171.6 1.7 convolution_convert_fusion.2
  173.3 2.1 convolution_convert_fusion
  175.5 15.3 %reduce-scatter.9.cloned.1.call-done = bf16[128,1024]{1,0:T(8,128)(2,1)} async-done(((bf16[512,1024]{1,0:T(8,128)(2,1)}), bf16[128,1024]{1,0:T(8,128)(2,1)}) %reduce-scatter.9.cloned.1.call-update) | async-done | bytes 262160 | tf_op jit(solution)/shard_map/reduce_scatter | solution.py:70
  190.8 1.0 convert_element_type.258
  192.1 42.8 %psum.28 = f32[16,128]{1,0:T(8,128)S(1)} all-reduce(f32[16,128]{1,0:T(8,128)S(1)} %pad_maximum_fusion.9), channel_id=1, replica_groups=mesh['dp'=8,'tensor'=4] {'dp','tensor'}, use_global_device_ids=true, to_apply=%region_19.20 | all-reduce | flops 2048 | bytes 16384 | tf_op jit(solution)/shard_map/psum | solution.py:285
  235.5 97.5 %all-reduce.4.cloned.1.call-done = (bf16[1024,512]{1,0:T(8,128)(2,1)}, bf16[512,1024]{1,0:T(8,128)(2,1)}, bf16[1024,640]{1,0:T(8,128)(2,1)}) async-done(((bf16[1024,512]{1,0:T(8,128)(2,1)}, bf16[512,1024]{1,0:T(8,128)(2,1)}, bf16[1024,640]{1,0:T(8,128)(2,1)}), (bf16[1024,512]{1,0:T(8,128)(2,1)}, bf16[512,1024]{1,0:T(8,128)(2,1)}, bf16[1024,640]{1,0:T(8,128)(2,1)})) %all-reduce.4.cloned.1.call-update) | async-done | bytes 3407888 | tf_op jit(solution)/shard_map/psum | solution.py:286
  333.1 1.8 slice.223
  334.9 1.6 convert_element_type.266
  336.5 1.0 slice.217
  337.5 1.9 copy.94
  339.5 1.5 pad_maximum_fusion.1
  341.2 1.0 fusion.94
  342.9 1.6 fusion.93
  344.4 15.0 %reduce-scatter.11.cloned.1.call-done = bf16[128,1024]{1,0:T(8,128)(2,1)} async-done(((bf16[512,1024]{1,0:T(8,128)(2,1)}), bf16[128,1024]{1,0:T(8,128)(2,1)}) %reduce-scatter.11.cloned.1.call-update) | async-done | bytes 262160 | tf_op jit(solution)/shard_map/reduce_scatter | solution.py:70
  359.5 2.2 fusion.36
  (199 shorter events, 16.6 us)
Async XLA Ops:
  7.2 37.1 %copy-start = (bf16[256,1024]{1,0:T(8,128)(2,1)S(1)}, bf16[256,1024]{1,0:T(8,128)(2,1)}, u32[]{:S(2)}) copy-start(bf16[256,1024]{1,0:T(8,128)(2,1)} %param.30) | copy-start | bytes 1572868
  7.2 4.5 %copy-start.46 = (s32[1,512]{1,0:T(1,128)S(1)}, s32[1,512]{1,0:T(1,128)}, u32[]{:S(2)}) copy-start(s32[1,512]{1,0:T(1,128)} %param.24) | copy-start | bytes 6148
  7.2 29.6 %copy-start.17 = (bf16[1024,256]{1,0:T(8,128)(2,1)S(1)}, bf16[1024,256]{1,0:T(8,128)(2,1)}, u32[]{:S(2)}) copy-start(bf16[1024,256]{1,0:T(8,128)(2,1)} %param.27) | copy-start | bytes 1572868
  7.2 29.6 %all-gather.4.cloned.1.call-start = ((), (), s32[]{:S(2)}) async-start(), calls=%async_computation.4 | async-start | bytes 2621440 | tf_op jit(solution)/shard_map/all_gather | solution.py:114
  8.4 30.2 %copy-start.52 = (f32[128]{0:T(128)}, f32[128]{0:T(128)S(1)}, u32[]{:S(2)}) copy-start(f32[128]{0:T(128)S(1)} %add_rsqrt_fusion.1) | copy-start | bytes 1540
  11.3 27.4 %copy-start.15 = (bf16[1024,128]{1,0:T(8,128)(2,1)S(1)}, bf16[1024,128]{1,0:T(8,128)(2,1)}, u32[]{:S(2)}) copy-start(bf16[1024,128]{1,0:T(8,128)(2,1)} %param.28) | copy-start | bytes 786436
  11.3 59.4 %reduce-scatter.5.cloned.1.call-start = ((), (), s32[]{:S(2)}) async-start(), calls=%async_computation.5 | async-start | bytes 1310720 | tf_op jit(solution)/shard_map/reduce_scatter | solution.py:70
  36.8 2.0 copy-start.22
  40.3 2.0 copy-start.8
  41.4 2.1 copy-start.47
  43.6 2.2 copy-start.54
  43.6 27.1 %copy-start.1 = (bf16[128,1024]{1,0:T(8,128)(2,1)S(1)}, bf16[128,1024]{1,0:T(8,128)(2,1)}, u32[]{:S(2)}) copy-start(bf16[128,1024]{1,0:T(8,128)(2,1)} %param.22) | copy-start | bytes 786436
  43.6 28.8 %copy-start.41 = (f32[1024]{0:T(1024)S(1)}, f32[1024]{0:T(1024)}, u32[]{:S(2)}) copy-start(f32[1024]{0:T(1024)} %param.31) | copy-start | bytes 12292
  44.2 29.2 %copy-start.31 = (bf16[1024,32]{0,1:T(8,128)(2,1)S(1)}, bf16[1024,32]{0,1:T(8,128)(2,1)}, u32[]{:S(2)}) copy-start(bf16[1024,32]{0,1:T(8,128)(2,1)} %param.32) | copy-start | bytes 196612
  45.7 48.3 %copy-start.25 = (bf16[2,1024,128]{2,1,0:T(8,128)(2,1)S(1)}, bf16[2,1024,128]{2,1,0:T(8,128)(2,1)}, u32[]{:S(2)}) copy-start(bf16[2,1024,128]{2,1,0:T(8,128)(2,1)} %param.34) | copy-start | bytes 1572868
  45.7 47.0 %all-gather.6.cloned.1.call-start = ((), (), s32[]{:S(2)}) async-start(), calls=%async_computation.6 | async-start | bytes 1474560 | tf_op jit(solution)/shard_map/all_gather | solution.py:160
  75.1 58.8 %reduce-scatter.7.cloned.1.call-start = ((), (), s32[]{:S(2)}) async-start(), calls=%async_computation.7 | async-start | bytes 1474560 | tf_op jit(solution)/shard_map/reduce_scatter | solution.py:70
  92.7 3.2 copy-start.43
  93.7 2.7 copy-start.23
  93.7 2.7 copy-start.36
  94.1 6.6 %copy-start.55 = (f32[512]{0:T(512)}, f32[512]{0:T(512)S(1)}, u32[]{:S(2)}) copy-start(f32[512]{0:T(512)S(1)} %get-tuple-element.98) | copy-start | bytes 6148
  94.1 6.6 %copy-start.57 = (f32[512]{0:T(512)}, f32[512]{0:T(512)S(1)}, u32[]{:S(2)}) copy-start(f32[512]{0:T(512)S(1)} %get-tuple-element.99) | copy-start | bytes 6148
  100.1 2.4 copy-start.37
  100.2 2.3 copy-start.59
  100.6 3.4 copy-start.26
  105.1 30.1 %copy-start.2 = (bf16[128,1024]{1,0:T(8,128)(2,1)S(1)}, bf16[128,1024]{1,0:T(8,128)(2,1)}, u32[]{:S(2)}) copy-start(bf16[128,1024]{1,0:T(8,128)(2,1)} %reduce-scatter.5.cloned.1.call-done) | copy-start | bytes 786436
  108.1 27.2 %copy-start.50 = (f32[128]{0:T(128)S(1)}, f32[128]{0:T(128)}, u32[]{:S(2)}) copy-start(f32[128]{0:T(128)} %copy-done.49) | copy-start | bytes 1540
  108.1 27.6 %copy-start.13 = (bf16[128,1024]{1,0:T(8,128)(2,1)S(1)}, bf16[128,1024]{1,0:T(8,128)(2,1)}, u32[]{:S(2)}) copy-start(bf16[128,1024]{1,0:T(8,128)(2,1)} %param.23) | copy-start | bytes 786436
  108.1 46.8 %all-gather.8.cloned.1.call-start = ((), (), s32[]{:S(2)}) async-start(), calls=%async_computation.8 | async-start | bytes 1474560 | tf_op jit(solution)/shard_map/all_gather | solution.py:211
  135.3 19.6 %copy-start.30 = (bf16[2,64,2,512]{3,1,2,0:T(8,128)(2,1)S(1)}, bf16[2,64,2,512]{3,1,2,0:T(8,128)(2,1)}, u32[]{:S(2)}) copy-start(bf16[2,64,2,512]{3,1,2,0:T(8,128)(2,1)} %copy-done.29) | copy-start | bytes 786436
  136.4 20.2 %copy-start.48 = (f32[2,2,512]{2,1,0:T(2,128)S(1)}, f32[2,2,512]{2,1,0:T(2,128)}, u32[]{:S(2)}) copy-start(f32[2,2,512]{2,1,0:T(2,128)} %copy-done.47) | copy-start | bytes 24580
  137.3 53.5 %reduce-scatter.9.cloned.1.call-start = ((), (), s32[]{:S(2)}) async-start(), calls=%async_computation.9 | async-start | bytes 1310720 | tf_op jit(solution)/shard_map/reduce_scatter | solution.py:70
  156.6 3.6 copy-start.9
  156.6 3.6 copy-start.62
  160.2 3.0 copy-start.39
  165.8 3.5 copy-start.45
  165.8 167.2 %all-reduce.4.cloned.1.call-start = ((), (), s32[]{:S(2)}) async-start(), calls=%async_computation.11 | async-start | bytes 6815744 | tf_op jit(solution)/shard_map/psum | solution.py:286
  169.3 2.2 copy-start.24
  169.3 2.2 copy-start.40
  175.4 16.4 %copy-start.42 = (f32[1024]{0:T(1024)S(1)}, f32[1024]{0:T(1024)}, u32[]{:S(2)}) copy-start(f32[1024]{0:T(1024)} %param.26) | copy-start | bytes 12292
  175.4 16.4 %copy-start.53 = (f32[128]{0:T(128)S(1)}, f32[128]{0:T(128)}, u32[]{:S(2)}) copy-start(f32[128]{0:T(128)} %copy-done.52) | copy-start | bytes 1540
  175.4 184.0 %reduce-scatter.11.cloned.1.call-start = ((), (), s32[]{:S(2)}) async-start(), calls=%async_computation.10 | async-start | bytes 1310720 | tf_op jit(solution)/shard_map/reduce_scatter | solution.py:70
  191.8 141.3 %copy-start.6 = (f32[128,1024]{1,0:T(8,128)}, f32[128,1024]{1,0:T(8,128)S(1)}, u32[]{:S(2)}) copy-start(f32[128,1024]{1,0:T(8,128)S(1)} %convert_element_type.258) | copy-start | bytes 1572868
  342.9 16.6 %copy-start.3 = (bf16[128,1024]{1,0:T(8,128)(2,1)S(1)}, bf16[128,1024]{1,0:T(8,128)(2,1)}, u32[]{:S(2)}) copy-start(bf16[128,1024]{1,0:T(8,128)(2,1)} %reduce-scatter.5.cloned.1.call-done) | copy-start | bytes 786436
  342.9 16.6 %copy-start.5 = (f32[128,1024]{1,0:T(8,128)S(1)}, f32[128,1024]{1,0:T(8,128)}, u32[]{:S(2)}) copy-start(f32[128,1024]{1,0:T(8,128)} %copy-done.4) | copy-start | bytes 1572868
  342.9 16.6 %copy-start.7 = (f32[128,1024]{1,0:T(8,128)S(1)}, f32[128,1024]{1,0:T(8,128)}, u32[]{:S(2)}) copy-start(f32[128,1024]{1,0:T(8,128)} %copy-done.6) | copy-start | bytes 1572868
  342.9 16.6 %copy-start.14 = (bf16[128,1024]{1,0:T(8,128)(2,1)S(1)}, bf16[128,1024]{1,0:T(8,128)(2,1)}, u32[]{:S(2)}) copy-start(bf16[128,1024]{1,0:T(8,128)(2,1)} %param.23) | copy-start | bytes 786436
  342.9 16.6 %copy-start.51 = (f32[128]{0:T(128)S(1)}, f32[128]{0:T(128)}, u32[]{:S(2)}) copy-start(f32[128]{0:T(128)} %copy-done.49) | copy-start | bytes 1540
  (23 other events, 29.7 us)
Sparse Core Ops, SparseCore 0:
  11.5 25.2 all-gather.3
  45.8 24.8 reduce-scatter.4
  75.2 17.4 all-gather.5
  108.2 25.6 reduce-scatter.6
  137.4 17.4 all-gather.7
  166.0 24.7 reduce-scatter.8
  195.9 137.1 all-reduce.3
  335.6 23.7 reduce-scatter.10

commit v2 on v1

--- a/solution.py
+++ b/solution.py
@@ -1,6 +1,11 @@
+import functools
+import math
+
 import jax
 import jax.numpy as jnp
 from jax import lax
+from jax.experimental import pallas as pl
+from jax.experimental.pallas import tpu as pltpu
 from jax.sharding import PartitionSpec as P
 
 HEAD_SIZE = 64
@@ -80,6 +85,212 @@
         "qhgd,khd->hgqk", query_block, keys_part, preferred_element_type=jnp.float32
     ) * HEAD_SIZE ** (-0.5)
     return jnp.where(allowed[None, None], scores, NEGATIVE)
+
+
+MESH = pl.DeviceIdType.MESH
+
+
+def reduce_kernel(n, inner, tensor_size, *refs):
+    outer = n // inner
+    pieces, gain_ref = refs[0:3], refs[3]
+    gate_out, up_out, router_out, down_out, wo_out, wq_out, wk_out, wv_out, gain_out = refs[4:13]
+    first, held, second, full = refs[13:16], refs[16:19], refs[19:22], refs[22:25]
+    gain_t, gain_sum, gain_d = refs[25:28]
+    send1, recv1, send2, recv2, send3, recv3, send4, recv4 = refs[28:36]
+    gsend_t, grecv_t, gsend_d, grecv_d = refs[36:40]
+    me = lax.axis_index("dp")
+    mt = lax.axis_index("tensor")
+    y = me % inner
+    z = me // inner
+
+    def remote(src, dst, send, recv, dp_index, tensor_index):
+        copy = pltpu.make_async_remote_copy(
+            src_ref=src,
+            dst_ref=dst,
+            send_sem=send,
+            recv_sem=recv,
+            device_id=(dp_index, tensor_index),
+            device_id_type=MESH,
+        )
+        copy.start()
+        return copy
+
+    barrier = pltpu.get_barrier_semaphore()
+    for k in range(1, n):
+        pl.semaphore_signal(barrier, inc=1, device_id=((me + k) % n, mt), device_id_type=MESH)
+    for k in range(1, tensor_size):
+        pl.semaphore_signal(
+            barrier, inc=1, device_id=(me, (mt + k) % tensor_size), device_id_type=MESH
+        )
+    pl.semaphore_wait(barrier, n - 1 + tensor_size - 1)
+
+    gain_copies = [
+        remote(
+            gain_ref, gain_t.at[k - 1], gsend_t.at[k - 1], grecv_t.at[k - 1],
+            me, (mt + k) % tensor_size,
+        )
+        for k in range(1, tensor_size)
+    ]
+    copies1 = []
+    for p in range(3):
+        started = []
+        for k in range(1, inner):
+            to = (y + k) % inner
+            started.append(
+                remote(
+                    pieces[p].at[to], first[p].at[k - 1], send1.at[p, k - 1], recv1.at[p, k - 1],
+                    z * inner + to, mt,
+                )
+            )
+        copies1.append(started)
+    for copy in gain_copies:
+        copy.wait()
+    total = gain_ref[...]
+    for k in range(1, tensor_size):
+        total = total + gain_t[k - 1]
+    gain_sum[...] = total
+    gain_copies = [
+        remote(
+            gain_sum, gain_d.at[k - 1], gsend_d.at[k - 1], grecv_d.at[k - 1], (me + k) % n, mt
+        )
+        for k in range(1, n)
+    ]
+    copies2 = []
+    for p in range(3):
+        for copy in copies1[p]:
+            copy.wait()
+        for o in range(outer):
+            acc = pieces[p][y, o].astype(jnp.float32)
+            for k in range(1, inner):
+                acc = acc + first[p][k - 1, o].astype(jnp.float32)
+            held[p][o] = acc.astype(jnp.bfloat16)
+        started = []
+        for k in range(1, outer):
+            to = (z + k) % outer
+            started.append(
+                remote(
+                    held[p].at[to], second[p].at[k - 1], send2.at[p, k - 1], recv2.at[p, k - 1],
+                    to * inner + y, mt,
+                )
+            )
+        copies2.append(started)
+    copies3 = []
+    for p in range(3):
+        for copy in copies2[p]:
+            copy.wait()
+        acc = held[p][z].astype(jnp.float32)
+        for k in range(1, outer):
+            acc = acc + second[p][k - 1].astype(jnp.float32)
+        full[p][y, z] = acc.astype(jnp.bfloat16)
+        started = []
+        for k in range(1, outer):
+            started.append(
+                remote(
+                    full[p].at[y, z], full[p].at[y, z], send3.at[p, k - 1], recv3.at[p, k - 1],
+                    ((z + k) % outer) * inner + y, mt,
+                )
+            )
+        copies3.append(started)
+    copies4 = []
+    for p in range(3):
+        for copy in copies3[p]:
+            copy.wait()
+        started = []
+        for k in range(1, inner):
+            started.append(
+                remote(
+                    full[p].at[y], full[p].at[y], send4.at[p, k - 1], recv4.at[p, k - 1],
+                    z * inner + (y + k) % inner, mt,
+                )
+            )
+        copies4.append(started)
+    for copy in gain_copies:
+        copy.wait()
+    total = gain_sum[...]
+    for k in range(1, n):
+        total = total + gain_d[k - 1]
+    gain_out[...] = total
+
+    experts, _, hidden = gate_out.shape
+    down_rows = down_out.shape[0]
+    query_cols, key_cols = wq_out.shape[1], wk_out.shape[1]
+    for p in range(3):
+        for copy in copies4[p]:
+            copy.wait()
+        depth = full[p].shape[2]
+        for i in range(inner):
+            for o in range(outer):
+                block = full[p][i, o].astype(jnp.float32)
+                start = (i * outer + o) * depth
+                rows = slice(start, start + depth)
+                if p == 0:
+                    for e in range(experts):
+                        gate_out[e, rows, :] = block[:, e * hidden : (e + 1) * hidden]
+                        at = (experts + e) * hidden
+                        up_out[e, rows, :] = block[:, at : at + hidden]
+                    router_out[rows, :] = block[:, 2 * experts * hidden :]
+                elif p == 1:
+                    if start < down_rows:
+                        down_out[rows, :] = block
+                    else:
+                        wo_out[start - down_rows : start - down_rows + depth, :] = block
+                else:
+                    wq_out[rows, :] = block[:, :query_cols]
+                    wk_out[rows, :] = block[:, query_cols : query_cols + key_cols]
+                    wv_out[rows, :] = block[:, query_cols + key_cols :]
+
+
+def reduce_sums(ffn_sums, row_sums, attn_sums, gains, gate_shape, down_shape, query_shape, key_shape):
+    n = lax.axis_size("dp")
+    tensor_size = lax.axis_size("tensor")
+    inner = math.isqrt(n)
+    outer = n // inner
+    pieces = [
+        piece.reshape(inner, outer, piece.shape[0] // n, piece.shape[1])
+        for piece in (ffn_sums, row_sums, attn_sums)
+    ]
+    blocks = [piece.shape[2:] for piece in pieces]
+    down_rows = down_shape[0] * down_shape[1]
+    float_out = functools.partial(jax.ShapeDtypeStruct, dtype=jnp.float32)
+    out_shape = [
+        float_out(gate_shape),
+        float_out(gate_shape),
+        float_out((ffn_sums.shape[0], 128)),
+        float_out((down_rows, row_sums.shape[1])),
+        float_out((row_sums.shape[0] - down_rows, row_sums.shape[1])),
+        float_out(query_shape),
+        float_out(key_shape),
+        float_out(key_shape),
+        float_out(gains.shape),
+    ]
+    half = jnp.bfloat16
+    scratch = (
+        [pltpu.VMEM((inner - 1, outer) + block, half) for block in blocks]
+        + [pltpu.VMEM((outer,) + block, half) for block in blocks]
+        + [pltpu.VMEM((outer - 1,) + block, half) for block in blocks]
+        + [pltpu.VMEM((inner, outer) + block, half) for block in blocks]
+        + [
+            pltpu.VMEM((tensor_size - 1,) + gains.shape, jnp.float32),
+            pltpu.VMEM(gains.shape, jnp.float32),
+            pltpu.VMEM((n - 1,) + gains.shape, jnp.float32),
+        ]
+        + [pltpu.SemaphoreType.DMA((3, inner - 1))] * 2
+        + [pltpu.SemaphoreType.DMA((3, outer - 1))] * 4
+        + [pltpu.SemaphoreType.DMA((3, inner - 1))] * 2
+        + [pltpu.SemaphoreType.DMA((tensor_size - 1,))] * 2
+        + [pltpu.SemaphoreType.DMA((n - 1,))] * 2
+    )
+    vmem = pl.BlockSpec(memory_space=pltpu.VMEM)
+    return pl.pallas_call(
+        functools.partial(reduce_kernel, n, inner, tensor_size),
+        out_shape=out_shape,
+        in_specs=[vmem] * 4,
+        out_specs=[vmem] * 9,
+        scratch_shapes=scratch,
+        compiler_params=pltpu.CompilerParams(
+            collective_id=0, has_side_effects=True, vmem_limit_bytes=48 * 1024 * 1024
+        ),
+    )(*pieces, gains)
 
 
 def on_device(
@@ -282,25 +493,19 @@
     grad_in, grad_gain_attn = norm_backward(grad_normed_attn, unit_attn, inverse_attn, gain_attn)
     grad_in = grad_in + grad_after
     gains = jnp.concatenate([grad_gain_ffn, grad_gain_attn]).reshape(-1, 128)
-    gains = lax.psum(gains, ("dp", "tensor"))
-    ffn_sums, row_sums, attn_sums = lax.psum((ffn_sums, row_sums, attn_sums), "dp")
-    ffn_sums = ffn_sums.astype(jnp.float32)
-    row_sums = row_sums.astype(jnp.float32)
-    attn_sums = attn_sums.astype(jnp.float32)
-    hidden = w_gate.shape[2]
-    grad_gate = jnp.stack([ffn_sums[:, e * hidden : (e + 1) * hidden] for e in range(experts_win)])
-    grad_up = jnp.stack(
-        [ffn_sums[:, e * hidden : (e + 1) * hidden] for e in range(experts_win, 2 * experts_win)]
-    )
-    grad_router = ffn_sums[:, 2 * experts_win * hidden :]
-    query_cols = w_query.shape[1]
-    key_cols = key_matrix.shape[1]
-    grad_w_query = attn_sums[:, :query_cols]
-    grad_w_key = attn_sums[:, query_cols : query_cols + key_cols]
-    grad_w_value = attn_sums[:, query_cols + key_cols :]
-    down_rows = grad_down.shape[0]
-    grad_down = row_sums[:down_rows]
-    grad_w_out = row_sums[down_rows:]
+    (
+        grad_gate,
+        grad_up,
+        grad_router,
+        grad_down,
+        grad_w_out,
+        grad_w_query,
+        grad_w_key,
+        grad_w_value,
+        gains,
+    ) = reduce_sums(
+        ffn_sums, row_sums, attn_sums, gains, w_gate.shape, w_down.shape, w_query.shape, key_matrix.shape
+    )
     gains = gains.reshape(2, width)
     grad_gain_ffn, grad_gain_attn = gains[0], gains[1]
     grad_router = grad_router[:, : w_router.shape[1]]

time: 370 us -> 345 us (0.932)
  Pallas kernels: 0 us -> 121 us
  waiting for transfers between devices: 238 us -> 134 us
  blocking collectives: 42.8 us -> 0 us
    pallas_call x0 -> x1, Pallas kernels: none -> 121 us  [reduce_sums(): pl.pallas_call(functools.partial(reduce_kernel, n, inner, tensor_size), o...]
    psum x1 -> x0, waiting for transfers between devices: 97.5 us -> none  [on_device(): lax.psum((ffn_sums, row_sums, attn_sums), 'dp')]
    psum x1 -> x0, blocking collectives: 42.8 us -> none  [on_device(): gains = lax.psum(gains, ('dp', 'tensor'))]
    unnamed x127 -> x138, local copies, waits for them, and re-layouts: 6.04 us -> 13.4 us
    reduce_scatter x4, waiting for transfers between devices: 80.7 us -> 73.6 us  [scatter_sum(): lax.psum_scatter(part.astype(jnp.bfloat16), 'tensor', scatter_dimension=0...]
    slice x4 -> x0, local copies, waits for them, and re-layouts: 5.41 us -> none  [the longest x1 1.78 us: on_device(): grad_router = grad_router[:, :w_router.shape[1]]]
  transfers between devices with their start and end apart: 8 -> 7, of which waited for: 8 -> 6; matrix products, arithmetic and copies ran while one was open for 6% -> 4% of each run, Pallas kernels for 0% -> 35%
where the time goes in v2:
time: 345 us; the launch traced here: 344 us
  waiting for transfers between devices  134 us (39%)
  Pallas kernels  121 us (35%)
  matrix products  34.7 us (10%)
  local copies, waits for them, and re-layouts  22.5 us (7%)
  other arithmetic  16.4 us (5%)
  between operations  15.1 us (4%)
    pallas_call x1, Pallas kernels, reduce_sums(): pl.pallas_call(functools.partial(reduce_kernel, n, inner, tensor_size), o...  121 us
    reduce_scatter x4, waiting for transfers between devices, scatter_sum(): lax.psum_scatter(part.astype(jnp.bfloat16), 'tensor', scatter_dimension=0...  73.6 us
    all_gather x1, waiting for transfers between devices, on_device(): lax.all_gather(jnp.concatenate([attention_normed, cotangent], axis=1), 't...  24.8 us
    all_gather x1, waiting for transfers between devices, on_device(): lax.all_gather(beside(grad_after.astype(jnp.bfloat16), grad_logits), 'ten...  17.5 us
    all_gather x1, waiting for transfers between devices, on_device(): lax.all_gather(beside(normed_ffn, combine_bf), 'tensor', axis=0, tiled=True)  17.5 us
    unnamed x138, local copies, waits for them, and re-layouts  13.4 us
    dot_general x5, matrix products, inner_rows(): lax.dot_general(left_op, right_op, (((0,), (0,)), ((), ())), preferred_el...  9.09 us
    dot_general x11, matrix products, outer_columns(): lax.dot_general(left_op, right_op, (((1,), (1,)), ((), ())), preferred_el...  7.21 us
  transfers between devices with their start and end apart: 7, of which 6 were waited for; matrix products, arithmetic and copies ran while one was open for 4% of the time, Pallas kernels for 35%

profile of v2, /device:TPU:0, one launch (start us, length us, event | category | flops | bytes accessed | tf_op | source)
XLA Modules:
  0.0 343.8 jit_solution(2116204849020469478)
XLA Ops:
  7.3 1.2 fusion.38
  8.4 1.1 fusion.32
  9.5 1.8 pad_maximum_fusion.1
  11.9 24.8 %all-gather.4.cloned.1.call-done = bf16[512,2048]{1,0:T(8,128)(2,1)} async-done(((bf16[128,2048]{1,0:T(8,128)(2,1)}), bf16[512,2048]{1,0:T(8,128)(2,1)}) %all-gather.4.cloned.1.call-update) | async-done | bytes 2097168 | tf_op jit(solution)/shard_map/all_gather | solution.py:325
  36.8 1.9 fusion.18
  39.3 0.9 fusion.4
  40.3 0.9 exponential_reduce_fusion
  42.3 1.3 convolution_convert_fusion.7
  44.2 1.4 convolution_convert_fusion.1
  45.8 24.9 %reduce-scatter.5.cloned.1.call-done = bf16[128,1024]{1,0:T(8,128)(2,1)} async-done(((bf16[512,1024]{1,0:T(8,128)(2,1)}), bf16[128,1024]{1,0:T(8,128)(2,1)}) %reduce-scatter.5.cloned.1.call-update) | async-done | bytes 262160 | tf_op jit(solution)/shard_map/reduce_scatter | solution.py:75
  70.7 1.1 multiply_reduce_fusion.3
  72.4 1.1 multiply_convert_fusion
  74.3 0.8 concatenate.64
  75.2 17.5 %all-gather.6.cloned.1.call-done = bf16[512,1152]{1,0:T(8,128)(2,1)} async-done(((bf16[128,1152]{1,0:T(8,128)(2,1)}), bf16[512,1152]{1,0:T(8,128)(2,1)}) %all-gather.6.cloned.1.call-update) | async-done | bytes 1179664 | tf_op jit(solution)/shard_map/all_gather | solution.py:371
  92.7 1.0 slice_convert_fusion
  94.1 1.8 fusion.30
  100.7 1.8 fusion.8
  102.4 0.8 stack.12
  105.1 2.9 concatenate.65
  108.4 25.5 %reduce-scatter.7.cloned.1.call-done = bf16[128,1152]{1,0:T(8,128)(2,1)} async-done(((bf16[512,1152]{1,0:T(8,128)(2,1)}), bf16[128,1152]{1,0:T(8,128)(2,1)}) %reduce-scatter.7.cloned.1.call-update) | async-done | bytes 294928 | tf_op jit(solution)/shard_map/reduce_scatter | solution.py:75
  133.9 1.0 convert_element_type.239
  136.4 0.8 concatenate.67
  137.3 17.5 %all-gather.8.cloned.1.call-done = bf16[512,1152]{1,0:T(8,128)(2,1)} async-done(((bf16[128,1152]{1,0:T(8,128)(2,1)}), bf16[512,1152]{1,0:T(8,128)(2,1)}) %all-gather.8.cloned.1.call-update) | async-done | bytes 1179664 | tf_op jit(solution)/shard_map/all_gather | solution.py:422
  154.9 1.7 multiply_reduce_fusion.1
  156.6 3.5 %fusion.9 = bf16[2,64,512]{2,1,0:T(8,128)(2,1)S(1)} fusion(bf16[512,2,2,64]{0,3,2,1:T(8,128)(2,1)S(1)} %bitcast.167, f32[2,512,512,2]{2,1,3,0:T(8,128)} %copy-done.13, f32[2,2,512]{2,1,0:T(2,128)S(1)} %copy-done.50, pred[512,512]{0,1:T(8,128)(4,1)S(1)} %fusion.10), kind=kOutput, calls=%fused_computation.31 | convolution fusion | flops 138477568 | bytes 4857856 | tf_op jit(solution)/shard_map/hgqk,qhgd->khd/dot_general | solution.py:448
  160.2 1.6 fusion.2
  164.3 1.5 add_convert_fusion.1
  165.9 1.6 convolution_convert_fusion.4
  167.6 23.2 %reduce-scatter.9.cloned.1.call-done = bf16[128,1024]{1,0:T(8,128)(2,1)} async-done(((bf16[512,1024]{1,0:T(8,128)(2,1)}), bf16[128,1024]{1,0:T(8,128)(2,1)}) %reduce-scatter.9.cloned.1.call-update) | async-done | bytes 262160 | tf_op jit(solution)/shard_map/reduce_scatter | solution.py:75
  190.8 1.0 convert_element_type.253
  191.9 1.8 convolution_convert_fusion.5
  193.7 1.8 convolution_convert_fusion.3
  195.5 1.0 pad_maximum_fusion
  196.6 0.9 slice_dynamic-update-slice_fusion
  197.5 1.7 convolution_convert_fusion.2
  199.3 2.1 convolution_convert_fusion
  201.7 121.0 %shard_map.239 = (f32[2,1024,128]{2,1,0:T(8,128)S(1)}, f32[2,1024,128]{2,1,0:T(8,128)S(1)}, f32[1024,128]{1,0:T(8,128)S(1)}, f32[256,1024]{1,0:T(8,128)S(1)}, f3...) custom-call(bf16[2,4,128,640]{3,2,1,0:T(8,128)(2,1)} %bitcast.147, ...), custom_call_target="tpu_custom_call" | custom-call | tf_op jit(solution)/shard_map/pallas_call | solution.py:284
  322.7 1.0 copy-done.1
  323.7 1.0 copy-done.3
  326.2 0.8 copy.94
  327.7 2.8 fusion.36
  330.5 1.0 copy.120
  331.5 0.8 copy.121
  332.2 0.8 copy.122
  333.0 1.0 copy.123
  334.0 1.0 copy.124
  335.0 1.0 copy.125
  336.0 1.0 copy.126
  (200 shorter events, 18.2 us)
Async XLA Ops:
  7.2 37.1 %copy-start = (bf16[256,1024]{1,0:T(8,128)(2,1)S(1)}, bf16[256,1024]{1,0:T(8,128)(2,1)}, u32[]{:S(2)}) copy-start(bf16[256,1024]{1,0:T(8,128)(2,1)} %param.30) | copy-start | bytes 1572868
  7.2 4.5 %copy-start.48 = (s32[1,512]{1,0:T(1,128)S(1)}, s32[1,512]{1,0:T(1,128)}, u32[]{:S(2)}) copy-start(s32[1,512]{1,0:T(1,128)} %param.24) | copy-start | bytes 6148
  7.2 29.6 %copy-start.19 = (bf16[1024,256]{1,0:T(8,128)(2,1)S(1)}, bf16[1024,256]{1,0:T(8,128)(2,1)}, u32[]{:S(2)}) copy-start(bf16[1024,256]{1,0:T(8,128)(2,1)} %param.27) | copy-start | bytes 1572868
  7.2 29.6 %all-gather.4.cloned.1.call-start = ((), (), s32[]{:S(2)}) async-start(), calls=%async_computation.4 | async-start | bytes 2621440 | tf_op jit(solution)/shard_map/all_gather | solution.py:325
  8.4 30.2 %copy-start.54 = (f32[128]{0:T(128)}, f32[128]{0:T(128)S(1)}, u32[]{:S(2)}) copy-start(f32[128]{0:T(128)S(1)} %add_rsqrt_fusion.1) | copy-start | bytes 1540
  11.3 27.4 %copy-start.17 = (bf16[1024,128]{1,0:T(8,128)(2,1)S(1)}, bf16[1024,128]{1,0:T(8,128)(2,1)}, u32[]{:S(2)}) copy-start(bf16[1024,128]{1,0:T(8,128)(2,1)} %param.28) | copy-start | bytes 786436
  11.3 59.4 %reduce-scatter.5.cloned.1.call-start = ((), (), s32[]{:S(2)}) async-start(), calls=%async_computation.5 | async-start | bytes 1310720 | tf_op jit(solution)/shard_map/reduce_scatter | solution.py:75
  41.4 2.1 copy-start.49
  43.5 2.2 copy-start.56
  43.6 27.1 %copy-start.9 = (bf16[128,1024]{1,0:T(8,128)(2,1)S(1)}, bf16[128,1024]{1,0:T(8,128)(2,1)}, u32[]{:S(2)}) copy-start(bf16[128,1024]{1,0:T(8,128)(2,1)} %param.22) | copy-start | bytes 786436
  43.6 28.8 %copy-start.44 = (f32[1024]{0:T(1024)S(1)}, f32[1024]{0:T(1024)}, u32[]{:S(2)}) copy-start(f32[1024]{0:T(1024)} %param.31) | copy-start | bytes 12292
  44.2 29.2 %copy-start.34 = (bf16[1024,32]{0,1:T(8,128)(2,1)S(1)}, bf16[1024,32]{0,1:T(8,128)(2,1)}, u32[]{:S(2)}) copy-start(bf16[1024,32]{0,1:T(8,128)(2,1)} %param.32) | copy-start | bytes 196612
  45.7 48.4 %copy-start.27 = (bf16[2,1024,128]{2,1,0:T(8,128)(2,1)S(1)}, bf16[2,1024,128]{2,1,0:T(8,128)(2,1)}, u32[]{:S(2)}) copy-start(bf16[2,1024,128]{2,1,0:T(8,128)(2,1)} %param.34) | copy-start | bytes 1572868
  45.7 47.0 %all-gather.6.cloned.1.call-start = ((), (), s32[]{:S(2)}) async-start(), calls=%async_computation.6 | async-start | bytes 1474560 | tf_op jit(solution)/shard_map/all_gather | solution.py:371
  75.1 58.7 %reduce-scatter.7.cloned.1.call-start = ((), (), s32[]{:S(2)}) async-start(), calls=%async_computation.7 | async-start | bytes 1474560 | tf_op jit(solution)/shard_map/reduce_scatter | solution.py:75
  92.7 3.2 copy-start.46
  93.8 2.7 copy-start.25
  93.8 2.7 copy-start.39
  94.1 6.6 %copy-start.57 = (f32[512]{0:T(512)}, f32[512]{0:T(512)S(1)}, u32[]{:S(2)}) copy-start(f32[512]{0:T(512)S(1)} %get-tuple-element.116) | copy-start | bytes 6148
  94.1 6.6 %copy-start.59 = (f32[512]{0:T(512)}, f32[512]{0:T(512)S(1)}, u32[]{:S(2)}) copy-start(f32[512]{0:T(512)S(1)} %get-tuple-element.117) | copy-start | bytes 6148
  100.1 2.3 copy-start.40
  100.2 2.2 copy-start.61
  100.7 3.4 copy-start.28
  105.1 30.1 %copy-start.10 = (bf16[128,1024]{1,0:T(8,128)(2,1)S(1)}, bf16[128,1024]{1,0:T(8,128)(2,1)}, u32[]{:S(2)}) copy-start(bf16[128,1024]{1,0:T(8,128)(2,1)} %reduce-scatter.5.cloned.1.call-done) | copy-start | bytes 786436
  108.1 27.2 %copy-start.52 = (f32[128]{0:T(128)S(1)}, f32[128]{0:T(128)}, u32[]{:S(2)}) copy-start(f32[128]{0:T(128)} %copy-done.51) | copy-start | bytes 1540
  108.1 27.6 %copy-start.15 = (bf16[128,1024]{1,0:T(8,128)(2,1)S(1)}, bf16[128,1024]{1,0:T(8,128)(2,1)}, u32[]{:S(2)}) copy-start(bf16[128,1024]{1,0:T(8,128)(2,1)} %param.23) | copy-start | bytes 786436
  108.1 46.8 %all-gather.8.cloned.1.call-start = ((), (), s32[]{:S(2)}) async-start(), calls=%async_computation.8 | async-start | bytes 1474560 | tf_op jit(solution)/shard_map/all_gather | solution.py:422
  135.2 19.6 %copy-start.32 = (bf16[2,64,2,512]{3,1,2,0:T(8,128)(2,1)S(1)}, bf16[2,64,2,512]{3,1,2,0:T(8,128)(2,1)}, u32[]{:S(2)}) copy-start(bf16[2,64,2,512]{3,1,2,0:T(8,128)(2,1)} %copy-done.31) | copy-start | bytes 786436
  136.4 20.2 %copy-start.50 = (f32[2,2,512]{2,1,0:T(2,128)S(1)}, f32[2,2,512]{2,1,0:T(2,128)}, u32[]{:S(2)}) copy-start(f32[2,2,512]{2,1,0:T(2,128)} %copy-done.49) | copy-start | bytes 24580
  137.3 53.5 %reduce-scatter.9.cloned.1.call-start = ((), (), s32[]{:S(2)}) async-start(), calls=%async_computation.9 | async-start | bytes 1310720 | tf_op jit(solution)/shard_map/reduce_scatter | solution.py:75
  156.6 3.5 %copy-start.14 = (f32[2,512,512,2]{2,1,3,0:T(8,128)S(1)}, f32[2,512,512,2]{2,1,3,0:T(8,128)}, u32[]{:S(2)}) copy-start(f32[2,512,512,2]{2,1,3,0:T(8,128)} %copy-done.13) | copy-start | bytes 12582916
  156.6 3.5 %copy-start.64 = (bf16[512,128]{0,1:T(8,128)(2,1)S(1)}, bf16[512,128]{0,1:T(8,128)(2,1)}, u32[]{:S(2)}) copy-start(bf16[512,128]{0,1:T(8,128)(2,1)} %copy-done.63) | copy-start | bytes 393220
  160.1 3.0 copy-start.42
  165.8 26.0 %copy-start.23 = (bf16[512,128]{1,0:T(8,128)(2,1)S(1)}, bf16[512,128]{1,0:T(8,128)(2,1)}, u32[]{:S(2)}) copy-start(bf16[512,128]{1,0:T(8,128)(2,1)} %copy-done.22) | copy-start | bytes 393220
  165.8 26.0 %copy-start.58 = (f32[512]{0:T(512)S(1)}, f32[512]{0:T(512)}, u32[]{:S(2)}) copy-start(f32[512]{0:T(512)} %copy-done.57) | copy-start | bytes 6148
  165.8 161.8 %reduce-scatter.11.cloned.1.call-start = ((), (), s32[]{:S(2)}) async-start(), calls=%async_computation.10 | async-start | bytes 1310720 | tf_op jit(solution)/shard_map/reduce_scatter | solution.py:75
  167.5 26.1 %copy-start.33 = (bf16[2,64,2,512]{3,1,2,0:T(8,128)(2,1)S(1)}, bf16[2,64,2,512]{3,1,2,0:T(8,128)(2,1)}, u32[]{:S(2)}) copy-start(bf16[2,64,2,512]{3,1,2,0:T(8,128)(2,1)} %copy-done.31) | copy-start | bytes 786436
  191.8 9.6 %copy-start.12 = (f32[128,1024]{1,0:T(8,128)}, f32[128,1024]{1,0:T(8,128)S(1)}, u32[]{:S(2)}) copy-start(f32[128,1024]{1,0:T(8,128)S(1)} %convert_element_type.253) | copy-start | bytes 1572868
  193.7 2.9 copy-start.62
  193.7 3.8 %copy-start.26 = (bf16[512,2048]{1,0:T(8,128)(2,1)S(1)}, bf16[512,2048]{1,0:T(8,128)(2,1)}, u32[]{:S(2)}) copy-start(bf16[512,2048]{1,0:T(8,128)(2,1)} %all-gather.4.cloned.1.call-done) | copy-start | bytes 6291460
  193.7 3.8 %copy-start.43 = (bf16[2,64,512]{2,1,0:T(8,128)(2,1)S(1)}, bf16[2,64,512]{2,1,0:T(8,128)(2,1)}, u32[]{:S(2)}) copy-start(bf16[2,64,512]{2,1,0:T(8,128)(2,1)} %copy-done.42) | copy-start | bytes 393220
  199.3 2.1 copy-start.45
  199.3 2.1 copy-start.55
  201.7 126.0 %copy-start.53 = (f32[128]{0:T(128)S(1)}, f32[128]{0:T(128)}, u32[]{:S(2)}) copy-start(f32[128]{0:T(128)} %copy-done.51) | copy-start | bytes 1540
  327.6 3.8 %copy-start.8 = (f32[1024,128]{1,0:T(8,128)S(1)}, f32[1024,128]{1,0:T(8,128)}, u32[]{:S(2)}) copy-start(f32[1024,128]{1,0:T(8,128)} %copy-done.7) | copy-start | bytes 1572868
  327.7 2.8 copy-start.16
  330.5 2.6 copy-start.4
  331.4 2.6 copy-start.2
  (24 other events, 28.8 us)
Sparse Core Ops, SparseCore 0:
  11.5 25.2 all-gather.3
  45.8 24.8 reduce-scatter.4
  75.3 17.4 all-gather.5
  108.2 25.6 reduce-scatter.6
  137.4 17.4 all-gather.7
  165.9 24.8 reduce-scatter.8
  193.9 24.8 reduce-scatter.10
